TPU v7x, 32 devices: a whole 2x2x4 slice. The times are simulated.
32 devices in a mesh: dp: 8 (over z, y), expert: 4 (over x, core).
Axes of the slice: x: 2, y: 2, z: 4, core: 2. Of those that a mesh axis runs over, the one named last changes fastest.
Arguments:
- grad_parts: bfloat16 [8, 12, 704, 2048], P('dp', 'expert'), may hold values from -90 to 90
- momentum: float32 [12, 704, 2048], P('expert', 'dp'), may hold values from -6 to 6
Outputs:
- new_momentum: float32 [12, 704, 2048], P('expert', 'dp')
- muon_update: float32 [12, 704, 2048], P('expert', 'dp')
All inputs are finite; a program needn't handle non-finite values.
Results may differ from a plain program's by a relative error of at most 0.023.
Values may be sent and summed in bfloat16 or wider, within the bound.
No kernel may reach another device: no remote copies, remote signals or barrier semaphores. Data moves between devices by JAX's collectives and lax.ppermute only.
A program may use at most 128 MiB of HBM per device.

v0:
```python
import math
import jax
import jax.numpy as jnp
from jax import lax
from jax.sharding import PartitionSpec as P

NS_ITERS = 3
momentum_decay = 0.95
coef_a = 3.4445
coef_b = -4.775
coef_c = 2.0315


def broadcast(x, axis, root):
    mine = lax.axis_index(axis) == root
    return lax.psum(jnp.where(mine, x, jnp.zeros_like(x)), axis)


def orthogonalize(direction):
    flat = direction.astype(jnp.float32)
    norm_value = jnp.sqrt(jnp.sum(flat * flat))
    current = (flat / (norm_value + 1e-07)).astype(jnp.bfloat16)
    for step in range(NS_ITERS):
        gram = jnp.dot(current, current.T, preferred_element_type=jnp.float32).astype(jnp.bfloat16)
        square = jnp.dot(gram, gram, preferred_element_type=jnp.float32)
        poly = (coef_b * gram.astype(jnp.float32) + coef_c * square).astype(jnp.bfloat16)
        current = (
            coef_a * current.astype(jnp.float32)
            + jnp.dot(poly, current, preferred_element_type=jnp.float32)
        ).astype(jnp.bfloat16)
    return current


def local(grad_parts, momentum):
    partials = grad_parts[0]
    matrix_count = partials.shape[0]
    rows_whole = partials.shape[1]
    columns = partials.shape[2]
    ranks = lax.axis_size("dp")
    stride = ranks // matrix_count
    owner_ranks = [matrix * stride for matrix in range(matrix_count)]
    dp_rank = lax.axis_index("dp")
    summed = lax.psum_scatter(partials, "dp", scatter_dimension=1, tiled=True).astype(jnp.float32)
    shard_rows = summed.shape[1]
    total_sq = lax.psum(jnp.sum(summed * summed), ("dp", "expert"))
    entry_count = matrix_count * lax.axis_size("expert") * rows_whole * columns
    factor = jnp.minimum(1.0, lax.rsqrt(total_sq / entry_count + 1e-06))
    scaled = factor * summed
    new_momentum = momentum_decay * momentum + scaled
    direction = (scaled + momentum_decay * new_momentum).astype(jnp.bfloat16)
    gathered = lax.all_gather(direction, "dp", axis=1, tiled=True)
    selector = jnp.stack([dp_rank == owner for owner in owner_ranks]).astype(jnp.bfloat16)
    owned = jnp.tensordot(selector, gathered, axes=1, preferred_element_type=jnp.float32).astype(
        jnp.bfloat16
    )
    result = orthogonalize(owned)
    blocks_out = []
    for owner in owner_ranks:
        broadcast_full = broadcast(result, "dp", owner)
        blocks_out.append(
            lax.dynamic_slice_in_dim(broadcast_full, dp_rank * shard_rows, shard_rows, 0)
        )
    ortho = jnp.stack(blocks_out)
    muon_update = 0.2 * math.sqrt(max(rows_whole, columns)) * ortho.astype(jnp.float32)
    return (new_momentum, muon_update)


def solution(mesh):
    return jax.shard_map(
        local,
        mesh=mesh,
        in_specs=(P("dp", "expert", None, None), P("expert", "dp", None)),
        out_specs=(P("expert", "dp", None), P("expert", "dp", None)),
        check_vma=False,
    )
```

profile of v0, /device:TPU:0, one launch (start us, length us, event | category | flops | bytes accessed | tf_op | source)
XLA Modules:
  0.0 731.8 jit_solution(7370153273644001469)
XLA Ops:
  7.2 13.6 %copy.6 = bf16[3,704,2048]{2,0,1:T(4,128)(2,1)} copy(bf16[3,704,2048]{2,1,0:T(8,128)(2,1)} %bitcast.42) | data formatting | bytes 17301504
  20.8 17.6 %copy.8 = bf16[88,8,3,2048]{3,1,2,0:T(8,128)(2,1)} copy(bf16[88,8,3,2048]{3,2,1,0:T(4,128)(2,1)} %bitcast.38) | data formatting | bytes 17301504
  38.4 0.5 all-gather.2.cloned.1.call-start
  38.9 155.8 %reduce-scatter.4.cloned.1.call-done = bf16[88,6144]{1,0:T(8,128)(2,1)} async-done(((bf16[704,6144]{1,0:T(8,128)(2,1)}), bf16[88,6144]{1,0:T(8,128)(2,1)}) %reduce-scatter.4.cloned.1.call-update) | async-done | bytes 1081360
  194.8 3.3 reshape.7
  198.1 1.3 fusion.7
  199.4 39.1 %psum.28 = f32[]{:T(128)} all-reduce(f32[]{:T(128)} %fusion.7), channel_id=1, replica_groups=mesh['dp'=8,'expert'=4] {'dp','expert'}, use_global_device_ids=true, to_apply=%region_2.0 | all-reduce | flops 1 | bytes 8 | tf_op jit(solution)/shard_map/psum | solution.py:45
  239.2 4.4 fusion.6
  243.6 0.0 all-reduce.3.cloned.1.call-start
  243.7 128.4 %all-gather.2.cloned.1.call-done = bf16[3,704,2048]{2,1,0:T(8,128)(2,1)} async-done(((bf16[3,88,2048]{2,1,0:T(8,128)(2,1)}), bf16[3,704,2048]{2,1,0:T(8,128)(2,1)}) %all-gather.2.cloned.1.call-update) | async-done | bytes 8650768 | tf_op jit(solution)/shard_map/all_gather | solution.py:51
  372.1 24.8 %fusion = bf16[1,704,2048]{2,0,1:T(2,128)(2,1)S(1)} fusion(bf16[3,704,2048]{2,1,0:T(8,128)(2,1)} %all-gather.2.cloned.1.call-done, pred[1]{0:T(512)(128)(4,1)} %bitcast.3, pred[1]{0:T(512)(128)(4,1)} %bitcast.2, pred[1]{0:T(512)(128)(4,1)} %bitcast.1), kind=kOutput, calls=%fused_computation | convolution fusion | flops 8650758 | bytes 11534339 | tf_op jit(solution)/shard_map/dot_general | solution.py:53
  396.9 2.5 copy-done
  399.4 3.4 fusion.2
  403.5 5.0 fusion.3
  408.4 3.4 convolution_convert_fusion.2
  411.8 7.0 add_convert_fusion.2
  418.8 6.1 convolution_convert_fusion.1
  424.9 7.3 add_convert_fusion.1
  432.2 3.4 convolution_convert_fusion
  435.6 9.2 %broadcast_select_fusion.2 = (bf16[704,2048]{1,0:T(8,128)(2,1)}, bf16[704,2048]{1,0:T(8,128)(2,1)}, bf16[704,2048]{1,0:T(8,128)(2,1)}) fusion(pred[]{:T(512)} %eq.12, pred[]{:T(512)} %eq.14, pred[]{:T(512)} %eq.13, bf16[704,2048]{1,0:T(8,128)(2,1)S(1)} %add_convert_fusion.1, bf16[704,704]{1,0:T(8,128)(2,1)} %convolution_convert_fusion), kind=kOutput, calls=%fused_computation.12 | convolution fusion | flops 2740441088 | bytes 12525571 | tf_op jit(solution)/shard_map/dot_general | solution.py:29
  444.8 276.5 %all-reduce.3.cloned.1.call-done = (bf16[704,2048]{1,0:T(8,128)(2,1)}, bf16[704,2048]{1,0:T(8,128)(2,1)}, bf16[704,2048]{1,0:T(8,128)(2,1)}) async-done(((bf16[704,2048]{1,0:T(8,128)(2,1)}, bf16[704,2048]{1,0:T(8,128)(2,1)}, bf16[704,2048]{1,0:T(8,128)(2,1)}), (bf16[704,2048]{1,0:T(8,128)(2,1)}, bf16[704,2048]{1,0:T(8,128)(2,1)}, bf16[704,2048]{1,0:T(8,128)(2,1)})) %all-reduce.3.cloned.1.call-update) | async-done | bytes 8650768 | tf_op jit(solution)/shard_map/psum | solution.py:16
  721.3 1.0 dynamic-slice_bitcast_fusion.2
  722.3 1.2 dynamic-slice_bitcast_fusion
  723.4 1.6 convert_multiply_fusion.3
  (5 shorter events, 0.1 us)
Async XLA Ops:
  7.2 187.6 %reduce-scatter.4.cloned.1.call-start = ((), (), s32[]{:S(2)}) async-start(), calls=%async_computation.2 | async-start | bytes 9732096
  38.4 333.7 %all-gather.2.cloned.1.call-start = ((), (), s32[]{:S(2)}) async-start(), calls=%async_computation.1 | async-start | bytes 9732096 | tf_op jit(solution)/shard_map/all_gather | solution.py:51
  243.6 477.6 %all-reduce.3.cloned.1.call-start = ((), (), s32[]{:S(2)}) async-start(), calls=%async_computation.3 | async-start | bytes 17301504 | tf_op jit(solution)/shard_map/psum | solution.py:16
  396.9 2.5 copy-start
Sparse Core Ops, SparseCore 0:
  38.5 156.1 reduce-scatter.3
  243.7 128.3 all-gather.1
  444.9 276.3 all-reduce.2
where the time goes:
time: 741 us; the launch traced here: 732 us
  waiting for transfers between devices  561 us (76%)
  matrix products  61.1 us (8%)
  local copies, waits for them, and re-layouts  39.1 us (5%)
  blocking collectives  39.1 us (5%)
  other arithmetic  15.7 us (2%)
  between operations  15.4 us (2%)
    psum x1, waiting for transfers between devices, broadcast(): return lax.psum(jnp.where(mine, x, jnp.zeros_like(x)), axis)  276 us
    unnamed x4, waiting for transfers between devices  156 us
    all_gather x1, waiting for transfers between devices, local(): gathered = lax.all_gather(direction, 'dp', axis=1, tiled=True)  128 us
    psum x1, blocking collectives, local(): total_sq = lax.psum(jnp.sum(summed * summed), ('dp', 'expert'))  39.1 us
    unnamed x5, local copies, waits for them, and re-layouts  36.9 us
    dot_general x1, matrix products, local(): jnp.tensordot(selector, gathered, axes=1, preferred_element_type=jnp.floa...  24.8 us
    dot_general x3, matrix products, orthogonalize(): jnp.dot(poly, current, preferred_element_type=jnp.float32)  23.4 us
  transfers between devices with their start and end apart: 3, of which 3 were waited for; matrix products, arithmetic and copies ran while one was open for 0% of the time, Pallas kernels for 0%

commit v1 on v0

--- a/solution.py
+++ b/solution.py
@@ -13,7 +13,7 @@
 
 def broadcast(x, axis, root):
     mine = lax.axis_index(axis) == root
-    return lax.psum(jnp.where(mine, x, jnp.zeros_like(x)), axis)
+    return jnp.sum(lax.all_gather(jnp.where(mine, x, jnp.zeros_like(x)), axis), axis=0)
 
 
 def orthogonalize(direction):

time: 741 us -> 1800 us (2.43)
  waiting for transfers between devices: 561 us -> 1580 us
  other arithmetic: 15.7 us -> 58.6 us
    all_gather x0 -> x3, waiting for transfers between devices: none -> 1300 us  [broadcast(): lax.all_gather(jnp.where(mine, x, jnp.zeros_like(x)), axis)]
    psum x1 -> x0, waiting for transfers between devices: 276 us -> none  [broadcast(): return lax.psum(jnp.where(mine, x, jnp.zeros_like(x)), axis)]
    reduce_sum x0 -> x3, other arithmetic: none -> 42.9 us  [broadcast(): jnp.sum(lax.all_gather(jnp.where(mine, x, jnp.zeros_like(x)), axis), axis=0)]
    unnamed x4 -> x6, waiting for transfers between devices: 156 us -> 157 us
  transfers between devices with their start and end apart: 3 -> 5, of which waited for: 3 -> 5; matrix products, arithmetic and copies ran while one was open for 0% -> 2% of each run, Pallas kernels for 0% -> 0%
where the time goes in v1:
time: 1800 us; the launch traced here: 1790 us
  waiting for transfers between devices  1580 us (88%)
  matrix products  60.6 us (3%)
  other arithmetic  58.6 us (3%)
  blocking collectives  39.1 us (2%)
  local copies, waits for them, and re-layouts  38.1 us (2%)
    all_gather x3, waiting for transfers between devices, broadcast(): lax.all_gather(jnp.where(mine, x, jnp.zeros_like(x)), axis)  1300 us
    unnamed x6, waiting for transfers between devices  157 us
    all_gather x1, waiting for transfers between devices, local(): gathered = lax.all_gather(direction, 'dp', axis=1, tiled=True)  128 us
    reduce_sum x3, other arithmetic, broadcast(): jnp.sum(lax.all_gather(jnp.where(mine, x, jnp.zeros_like(x)), axis), axis=0)  42.9 us
    psum x1, blocking collectives, local(): total_sq = lax.psum(jnp.sum(summed * summed), ('dp', 'expert'))  39.1 us
    unnamed x5, local copies, waits for them, and re-layouts  36.9 us
  transfers between devices with their start and end apart: 5, of which 5 were waited for; matrix products, arithmetic and copies ran while one was open for 2% of the time, Pallas kernels for 0%

profile of v1, /device:TPU:0, one launch (start us, length us, event | category | flops | bytes accessed | tf_op | source)
XLA Modules:
  0.0 1793.0 jit_solution(6982704167929673978)
XLA Ops:
  7.2 13.6 copy.6
  20.8 17.6 copy.8
  38.9 155.9 %reduce-scatter.4.cloned.1.call-done = bf16[88,6144]{1,0:T(8,128)(2,1)} async-done(((bf16[704,6144]{1,0:T(8,128)(2,1)}), bf16[88,6144]{1,0:T(8,128)(2,1)}) %reduce-scatter.4.cloned.1.call-update) | async-done | bytes 1081360
  194.8 3.3 reshape.10
  199.4 39.1 %psum.7 = f32[]{:T(128)} all-reduce(f32[]{:T(128)} %fusion.7), channel_id=1, replica_groups=mesh['dp'=8,'expert'=4] {'dp','expert'}, use_global_device_ids=true, to_apply=%region_2.0 | all-reduce | flops 1 | bytes 8 | tf_op jit(solution)/shard_map/psum | solution.py:45
  239.2 4.4 fusion.6
  243.7 128.4 %all-gather.8.cloned.1.call-done = bf16[3,704,2048]{2,1,0:T(8,128)(2,1)} async-done(((bf16[3,88,2048]{2,1,0:T(8,128)(2,1)}), bf16[3,704,2048]{2,1,0:T(8,128)(2,1)}) %all-gather.8.cloned.1.call-update) | async-done | bytes 8650768 | tf_op jit(solution)/shard_map/all_gather | solution.py:51
  372.1 24.8 %fusion = bf16[1,704,2048]{2,0,1:T(2,128)(2,1)S(1)} fusion(bf16[3,704,2048]{2,1,0:T(8,128)(2,1)} %all-gather.8.cloned.1.call-done, pred[1]{0:T(512)(128)(4,1)} %bitcast.3, pred[1]{0:T(512)(128)(4,1)} %bitcast.2, pred[1]{0:T(512)(128)(4,1)} %bitcast.1), kind=kOutput, calls=%fused_computation | convolution fusion | flops 8650758 | bytes 11534339 | tf_op jit(solution)/shard_map/dot_general | solution.py:53
  396.9 2.5 copy-done
  399.4 3.4 fusion.2
  403.4 5.0 fusion.3
  408.4 3.4 convolution_convert_fusion.2
  411.8 6.7 add_convert_fusion.2
  418.6 6.1 convolution_convert_fusion.1
  424.7 7.2 add_convert_fusion.1
  431.9 3.4 convolution_convert_fusion
  435.3 9.0 broadcast_select_fusion.2
  445.4 438.3 %all-gather.10.cloned.1.call-done = bf16[5632,2048]{1,0:T(8,128)(2,1)} async-done(((bf16[704,2048]{1,0:T(8,128)(2,1)}), bf16[5632,2048]{1,0:T(8,128)(2,1)}) %all-gather.10.cloned.1.call-update) | async-done | bytes 23068688 | tf_op jit(solution)/shard_map/all_gather | solution.py:16
  883.7 13.4 reduce_sum.56
  897.1 429.2 %all-gather.14.cloned.1.call-done = bf16[5632,2048]{1,0:T(8,128)(2,1)} async-done(((bf16[704,2048]{1,0:T(8,128)(2,1)}), bf16[5632,2048]{1,0:T(8,128)(2,1)}) %all-gather.14.cloned.1.call-update) | async-done | bytes 23068688 | tf_op jit(solution)/shard_map/all_gather | solution.py:16
  1326.3 15.0 reduce_sum.58
  1341.3 427.6 %all-gather.12.cloned.1.call-done = bf16[5632,2048]{1,0:T(8,128)(2,1)} async-done(((bf16[704,2048]{1,0:T(8,128)(2,1)}), bf16[5632,2048]{1,0:T(8,128)(2,1)}) %all-gather.12.cloned.1.call-update) | async-done | bytes 23068688 | tf_op jit(solution)/shard_map/all_gather | solution.py:16
  1768.9 14.6 reduce_sum.57
  1784.7 1.6 convert_multiply_fusion.3
  (14 shorter events, 4.3 us)
Async XLA Ops:
  7.2 187.6 %reduce-scatter.4.cloned.1.call-start = ((), (), s32[]{:S(2)}) async-start(), calls=%async_computation.5 | async-start | bytes 9732096
  38.4 333.7 %all-gather.8.cloned.1.call-start = ((), (), s32[]{:S(2)}) async-start(), calls=%async_computation.1 | async-start | bytes 9732096 | tf_op jit(solution)/shard_map/all_gather | solution.py:51
  243.6 640.1 %all-gather.10.cloned.1.call-start = ((), (), s32[]{:S(2)}) async-start(), calls=%async_computation.2 | async-start | bytes 25952256 | tf_op jit(solution)/shard_map/all_gather | solution.py:16
  396.9 2.5 copy-start
  444.3 882.0 %all-gather.14.cloned.1.call-start = ((), (), s32[]{:S(2)}) async-start(), calls=%async_computation.4 | async-start | bytes 25952256 | tf_op jit(solution)/shard_map/all_gather | solution.py:16
  444.8 1324.0 %all-gather.12.cloned.1.call-start = ((), (), s32[]{:S(2)}) async-start(), calls=%async_computation.3 | async-start | bytes 25952256 | tf_op jit(solution)/shard_map/all_gather | solution.py:16
Sparse Core Ops, SparseCore 0:
  38.5 156.2 reduce-scatter.3
  243.7 128.3 all-gather.7
  444.4 439.2 all-gather.9
  885.2 441.0 all-gather.13
  1327.7 441.0 all-gather.11
